TPU v7x, 32 devices: a whole 2x2x4 slice. The times are simulated.
32 devices in a mesh: freq: 4 (over x, core), tile: 8 (over z, y).
Axes of the slice: x: 2, y: 2, z: 4, core: 2. Of those that a mesh axis runs over, the one named last changes fastest.
Arguments:
- plus_time: bfloat16 [128, 128, 12288], P('freq', None, 'tile'), may hold values from -6 to 6
- minus_time: bfloat16 [128, 128, 12288], P('freq', None, 'tile'), may hold values from -6 to 6
- gate_starts: int32 [128, 48], P('freq', 'tile'), may hold values from 0 to 64
- tile_ranks: int32 [4, 48, 48], P('freq', None, 'tile'), may hold values from 1 to 64, as said below
- u_factors: bfloat16 [4, 48, 48, 2, 64, 256], P('freq', 'tile'), may hold values from -0.109375 to 0.109375
- v_factors: bfloat16 [4, 48, 48, 2, 64, 256], P('freq', None, 'tile'), may hold values from -0.375 to 0.375
Outputs:
- minus_new: bfloat16 [4, 2, 128, 12288], P('freq', None, None, 'tile')
- plus_new: bfloat16 [4, 2, 128, 12288], P('freq', None, None, 'tile')
- cross_gram: float32 [4, 2, 128, 128], P('freq', None, 'tile')
- normal_gram: float32 [4, 2, 128, 128], P('freq', None, 'tile')
Inputs may be any that keep to these rules, and one draw needn't show every extreme that they name: `tile_ranks`: tiles with |i - j| <= 1 have rank 64; every other tile has rank at most 32, and some tile of every draw has exactly 32.
All inputs are finite; a program needn't handle non-finite values.
Results may differ from a plain program's by a relative error of at most 0.014.
Values may be sent and summed in bfloat16 or wider, within the bound.
A program may use at most 192 MiB of HBM per device.

v0:
```python
import math
import jax
import jax.numpy as jnp
from jax import lax
from jax.sharding import PartitionSpec as P

R = 12288
GATE = 64


def extended(x, sides, width):
    for axis, dim in sides:
        size, length = (lax.axis_size(axis), x.shape[dim])
        up = [(i, (i + 1) % size) for i in range(size - 1)]
        down = [(j, i) for i, j in up]
        last = lax.slice_in_dim(x, length - width, length, axis=dim)
        leading = lax.slice_in_dim(x, 0, width, axis=dim)
        before = lax.ppermute(last, axis, up)
        after = lax.ppermute(leading, axis, down)
        x = jnp.concatenate([before, x, after], axis=dim)
    return x


def make_table(freq_count, sample_count):
    freq_ids = lax.broadcasted_iota(jnp.int32, (freq_count, sample_count), 0)
    sample_ids = lax.broadcasted_iota(jnp.int32, (freq_count, sample_count), 1)
    phase_ids = freq_ids * sample_ids % sample_count
    angles = phase_ids.astype(jnp.float32) * (2.0 * math.pi / sample_count)
    amplitude = 1.0 / math.sqrt(GATE)
    return jnp.stack([jnp.cos(angles) * amplitude, -jnp.sin(angles) * amplitude]).astype(
        jnp.bfloat16
    )


def half_signs(entry_count):
    entry_ids = lax.broadcasted_iota(jnp.int32, (entry_count,), 0)
    return jnp.where(entry_ids < entry_count // 2, 1.0, -1.0).astype(jnp.float32)


def gate_field(traces, gate_starts):
    sources, samples, receivers = traces.shape
    blocks = gate_starts.shape[1]
    shaped = traces.reshape(sources, samples, blocks, receivers // blocks)
    sample_ids = lax.broadcasted_iota(jnp.int32, (1, samples, 1, 1), 1)
    starts = gate_starts[:, None, :, None]
    inside = (sample_ids >= starts) & (sample_ids < starts + GATE)
    kept = jnp.where(inside, shaped, jnp.zeros((), traces.dtype))
    return kept.reshape(sources, samples, receivers)


def on_device(plus_time, minus_time, gate_starts, tile_ranks, u_factors, v_factors):
    f_local = u_factors.shape[0]
    row_tiles = u_factors.shape[1]
    all_tiles = u_factors.shape[2]
    col_tiles = v_factors.shape[2]
    rank_depth = v_factors.shape[4]
    half_depth = rank_depth // 2
    freq_total = f_local * lax.axis_size("freq")
    sample_count = plus_time.shape[1]
    stacked = jnp.stack([gate_field(plus_time, gate_starts), gate_field(minus_time, gate_starts)])
    dft_table = make_table(freq_total, sample_count)
    local_spec = jnp.einsum(
        "cft,qstr->fcqsr", dft_table, stacked, preferred_element_type=jnp.float32
    ).astype(jnp.bfloat16)
    spectra = lax.all_to_all(local_spec, "freq", split_axis=0, concat_axis=3, tiled=True)
    both_sources = 2 * spectra.shape[3]
    columns = spectra.reshape(f_local, 2, both_sources, col_tiles, spectra.shape[4] // col_tiles)
    sign_vec = half_signs(both_sources)
    partial_c = jnp.einsum(
        "fijckr,fdsjr->fijcdks", v_factors, columns, preferred_element_type=jnp.float32
    )
    coeff_real = partial_c[:, :, :, 0, 0] - sign_vec * partial_c[:, :, :, 1, 1]
    coeff_imag = partial_c[:, :, :, 0, 1] + sign_vec * partial_c[:, :, :, 1, 0]
    rank_ids = lax.broadcasted_iota(jnp.int32, (1, 1, 1, rank_depth), 3)
    rank_mask = (rank_ids < tile_ranks[:, :, :, None]).astype(jnp.float32)[..., None]
    coeff_all = jnp.stack([coeff_real * rank_mask, coeff_imag * rank_mask], 3).astype(jnp.bfloat16)
    lower_part = coeff_all[:, :, :, :, :half_depth]
    lower_rows = lax.all_to_all(lower_part, "tile", split_axis=1, concat_axis=2, tiled=True)
    products = jnp.einsum(
        "fijckr,fijeks->fcesir",
        u_factors[:, :, :, :, :half_depth],
        lower_rows,
        preferred_element_type=jnp.float32,
    )
    block_start = lax.axis_index("tile") * col_tiles
    local_ids = lax.broadcasted_iota(jnp.int32, (col_tiles,), 0)
    global_cols = block_start + local_ids
    band_list = []
    for offset in (-1, 0, 1):
        band_rows = global_cols + offset
        valid = (band_rows >= 0) & (band_rows < all_tiles)
        clipped = jnp.clip(band_rows, 0, all_tiles - 1)
        picked = coeff_all[:, clipped, local_ids][:, :, :, half_depth:]
        band_list.append(
            jnp.where(valid[None, :, None, None, None], picked, jnp.zeros((), picked.dtype))
        )
    band_upper = jnp.stack(band_list, 1)
    padded_band = extended(band_upper, (("tile", 2),), 1)
    row_global = lax.axis_index("tile") * row_tiles + lax.broadcasted_iota(
        jnp.int32, (row_tiles,), 0
    )
    row_local = lax.broadcasted_iota(jnp.int32, (row_tiles,), 0)
    coeff_band = []
    u_band = []
    for position, offset in enumerate((-1, 0, 1)):
        coeff_band.append(padded_band[:, position, 1 - offset : 1 - offset + row_tiles])
        partner = jnp.clip(row_global - offset, 0, all_tiles - 1)
        u_band.append(u_factors[:, row_local, partner][:, :, :, half_depth:])
    band_products = jnp.einsum(
        "fdickr,fdieks->fcesir",
        jnp.stack(u_band, 1),
        jnp.stack(coeff_band, 1),
        preferred_element_type=jnp.float32,
    )
    products = products + band_products
    resp_real = products[:, 0, 0] - sign_vec[:, None, None] * products[:, 1, 1]
    resp_imag = products[:, 0, 1] + sign_vec[:, None, None] * products[:, 1, 0]
    response = jnp.stack([resp_real, resp_imag], 1).reshape(f_local, 2, both_sources, -1)
    rounded = response.astype(jnp.bfloat16)
    half_count = both_sources // 2
    minus_new = rounded[:, :, :half_count]
    plus_new = rounded[:, :, half_count:]
    gram_parts = jnp.einsum(
        "fczr,fesr->fczes", rounded, plus_new, preferred_element_type=jnp.float32
    )
    gram_real = gram_parts[:, 0, :, 0] + gram_parts[:, 1, :, 1]
    gram_imag = gram_parts[:, 1, :, 0] - gram_parts[:, 0, :, 1]
    row_ids = lax.broadcasted_iota(jnp.int32, (both_sources, 1), 0)
    row_scale = jnp.where(row_ids < half_count, 1.0 / math.sqrt(R), 1.0 / R).astype(jnp.float32)
    gram_all = jnp.stack([gram_real * row_scale, gram_imag * row_scale], 1)
    gram_all = gram_all.reshape(f_local, 2, 2, half_count, half_count).transpose(0, 2, 1, 3, 4)
    gram_total = lax.psum(gram_all.astype(jnp.bfloat16), "tile").astype(jnp.float32)
    row_share = half_count // lax.axis_size("tile")
    own_rows = lax.dynamic_slice_in_dim(
        gram_total, lax.axis_index("tile") * row_share, row_share, 3
    )
    return (minus_new, plus_new, own_rows[:, 0], own_rows[:, 1])


def solution(mesh):
    placed = (
        P("freq", None, "tile"),
        P("freq", None, "tile"),
        P("freq", "tile"),
        P("freq", None, "tile"),
        P("freq", "tile", None, None, None, None),
        P("freq", None, "tile", None, None, None),
    )
    return jax.shard_map(
        on_device,
        mesh=mesh,
        in_specs=placed,
        out_specs=(
            P("freq", None, None, "tile"),
            P("freq", None, None, "tile"),
            P("freq", None, "tile", None),
            P("freq", None, "tile", None),
        ),
        check_vma=False,
    )
```

profile of v0, /device:TPU:0, one launch (start us, length us, event | category | flops | bytes accessed | tf_op | source)
XLA Modules:
  0.0 496.3 jit_solution(5784172588843423811)
XLA Ops:
  8.9 4.3 broadcast_in_dim.81
  13.2 14.4 %copy.68 = pred[32,128,1536]{2,1,0:T(8,128)(4,1)} copy(pred[32,128,1536]{1,2,0:T(8,128)(4,1)} %bitcast.187) | data formatting | bytes 12582912 | tf_op jit(solution)/shard_map/jit(_where)/broadcast_in_dim | solution.py:47
  27.6 15.3 %select_bitcast_fusion.1 = (bf16[1,32,128,1536]{3,2,1,0:T(8,128)(2,1)S(1)}, bf16[1,32,128,1536]{3,2,1,0:T(8,128)(2,1)}) fusion(pred[32,128,1536]{2,1,0:T(8,128)(4,1)} %copy.68, bf16[32,128,1536]{2,1,0:T(8,128)(2,1)} %param.6, bf16[32,128,1536]{2,1,0:T(8,128)(2,1)} %param.7), kind=kLoop, calls=%fused_computation.27 | loop fusion | flops 12582912 | bytes 56623104 | tf_op jit(solution)/shard_map/jit(_where)/select_n | solution.py:47
  42.9 6.8 %fusion.18 = bf16[4,2,2,32,1536]{4,0,1,3,2:T(4,128)(2,1)S(1)} fusion(bf16[1,32,128,1536]{3,2,1,0:T(8,128)(2,1)} %get-tuple-element.11, bf16[1,32,128,1536]{3,2,1,0:T(8,128)(2,1)S(1)} %get-tuple-element.10, bf16[1,4,128]{2,1,0:T(4,128)(2,1)S(1)} %get-tuple-element.24, bf16[1,4,128]{2,1,0:T(4,128)(2,1)S(1)} %get-tuple-element.25), kind=kOutput, calls=%fused_computation.37 | convolution fusion | flops 252448768 | bytes 26740736 | tf_op jit(solution)/shard_map/cft,qstr->fcqsr/dot_general | solution.py:62
  52.1 4.2 all-to-all-start
  56.5 19.9 %all-to-all-done = bf16[4,2,2,32,1536]{4,1,3,2,0:T(2,128)(2,1)S(1)} async-done(((bf16[4,2,2,32,1536]{4,1,3,2,0:T(2,128)(2,1)}), bf16[4,2,2,32,1536]{4,1,3,2,0:T(2,128)(2,1)S(1)}, u32[]{:S(2)}, u32[]{:S(2)}) %all-to-all-start) | async-done | bytes 1572896 | tf_op jit(solution)/shard_map/all_to_all | solution.py:65
  81.1 32.4 %convolution_bitcast_fusion = f32[1,48,6,2,2,64,256]{6,5,3,1,4,2,0:T(8,128)} fusion(bf16[2,256,6,256,1,1]{3,2,1,0,5,4:T(8,128)(2,1)S(1)} %bitcast.189, bf16[1,48,6,2,64,256]{5,4,3,2,1,0:T(8,128)(2,1)} %param.11), kind=kOutput, calls=%fused_computation.6 | convolution fusion | flops 9663676416 | bytes 95944704 | tf_op jit(solution)/shard_map/fijckr,fdsjr->fijcdks/dot_general | solution.py:69
  113.5 24.0 %fusion.12 = (bf16[1,48,6,1,64,256]{5,4,1,2,3,0:T(8,128)(2,1)S(1)}, bf16[1,48,6,1,64,256]{5,4,1,2,3,0:T(8,128)(2,1)S(1)}) fusion(f32[1,48,6,2,2,64,256]{6,5,3,1,4,2,0:T(8,128)} %convolution_bitcast_fusion, f32[48,6,64]{2,0,1:T(8,128)S(1)} %fusion.49, f32[256]{0:T(256)S(1)} %compare_select_fusion.4), kind=kLoop, calls=%fused_computation.29 | loop fusion | flops 37748736 | bytes 94446592 | tf_op jit(solution)/shard_map/stack | solution.py:76
  143.9 4.1 fusion.13
  148.0 9.0 %copy.77 = bf16[1,48,6,2,32,256]{5,4,2,3,0,1:T(8,128)(2,1)} copy(bf16[1,48,6,2,32,256]{5,4,1,2,3,0:T(8,128)(2,1)} %fusion.13) | data formatting | bytes 18874368 | tf_op jit(solution)/shard_map/slice | solution.py:77
  157.0 6.6 %all-to-all-start.1 = ((bf16[1,48,6,2,32,256]{5,4,2,3,0,1:T(8,128)(2,1)}), bf16[1,48,6,2,32,256]{5,4,2,3,0,1:T(8,128)(2,1)}, u32[]{:S(2)}, u32[]{:S(2)}) async-start(bf16[1,48,6,2,32,256]{5,4,2,3,0,1:T(8,128)(2,1)} %copy.77), calls=%async_computation.1 | async-start | bytes 18874368 | tf_op jit(solution)/shard_map/all_to_all | solution.py:78
  163.7 6.9 %gather_fusion.5 = bf16[6,2,64,256]{3,2,1,0:T(8,128)(2,1)S(1)} fusion(bf16[6,48,2,64,256]{4,3,2,1,0:T(8,128)(2,1)} %bitcast.205, s32[6]{0:T(128)S(1)} %get-tuple-element.28), kind=kCustom, calls=%fused_computation.5 | custom fusion | bytes 786480 | tf_op jit(solution)/shard_map/gather | solution.py:108
  170.7 6.9 %gather_fusion.4 = bf16[6,2,64,256]{3,2,1,0:T(8,128)(2,1)S(1)} fusion(bf16[6,48,2,64,256]{4,3,2,1,0:T(8,128)(2,1)} %bitcast.206, s32[6]{0:T(128)S(1)} %get-tuple-element.29), kind=kCustom, calls=%fused_computation.4 | custom fusion | bytes 786480 | tf_op jit(solution)/shard_map/gather | solution.py:108
  177.6 6.9 %gather_fusion.3 = bf16[6,2,64,256]{3,2,1,0:T(8,128)(2,1)S(1)} fusion(bf16[6,48,2,64,256]{4,3,2,1,0:T(8,128)(2,1)} %bitcast.207, s32[6]{0:T(128)S(1)} %get-tuple-element.30), kind=kCustom, calls=%fused_computation.3 | custom fusion | bytes 786480 | tf_op jit(solution)/shard_map/gather | solution.py:108
  184.7 16.5 %fusion.1 = bf16[48,6,2,64,256]{4,3,0,1,2:T(8,128)(2,1)} fusion(bf16[1,48,6,1,64,256]{5,4,1,2,3,0:T(8,128)(2,1)} %copy-done, bf16[1,48,6,1,64,256]{5,4,1,2,3,0:T(8,128)(2,1)} %copy-done.1), kind=kLoop, calls=%fused_computation.12 | loop fusion | flops 9437184 | bytes 37748736 | tf_op jit(solution)/shard_map/stack | solution.py:76
  201.2 6.9 %gather_fusion.2 = bf16[6,2,64,256]{3,2,1,0:T(8,128)(2,1)S(1)} fusion(bf16[48,6,2,64,256]{4,3,0,1,2:T(8,128)(2,1)} %fusion.1, s32[6]{0:T(128)S(1)} %get-tuple-element.31), kind=kCustom, calls=%fused_computation.2 | custom fusion | bytes 786480 | tf_op jit(solution)/shard_map/gather | solution.py:93
  208.2 6.9 %gather_fusion.1 = bf16[6,2,64,256]{3,2,1,0:T(8,128)(2,1)S(1)} fusion(bf16[48,6,2,64,256]{4,3,0,1,2:T(8,128)(2,1)} %fusion.1, s32[6]{0:T(128)S(1)} %get-tuple-element.32), kind=kCustom, calls=%fused_computation.1 | custom fusion | bytes 786480 | tf_op jit(solution)/shard_map/gather | solution.py:93
  215.1 6.9 %gather_fusion = bf16[6,2,64,256]{3,2,1,0:T(8,128)(2,1)S(1)} fusion(bf16[48,6,2,64,256]{4,3,0,1,2:T(8,128)(2,1)} %fusion.1, s32[6]{0:T(128)S(1)} %get-tuple-element.33), kind=kCustom, calls=%fused_computation | custom fusion | bytes 786480 | tf_op jit(solution)/shard_map/gather | solution.py:93
  223.8 4.6 collective-permute-start.1
  228.3 141.7 %all-to-all-done.1 = bf16[1,48,6,2,32,256]{5,4,2,3,0,1:T(8,128)(2,1)} async-done(((bf16[1,48,6,2,32,256]{5,4,2,3,0,1:T(8,128)(2,1)}), bf16[1,48,6,2,32,256]{5,4,2,3,0,1:T(8,128)(2,1)}, u32[]{:S(2)}, u32[]{:S(2)}) %all-to-all-start.1) | async-done | bytes 9437216 | tf_op jit(solution)/shard_map/all_to_all | solution.py:78
  370.0 9.1 %copy.78 = bf16[1,48,6,2,32,256]{5,4,3,2,1,0:T(8,128)(2,1)} copy(bf16[1,48,6,2,32,256]{5,4,2,3,0,1:T(8,128)(2,1)} %all-to-all-done.1) | data formatting | bytes 18874368 | tf_op jit(solution)/shard_map/all_to_all | solution.py:78
  379.1 9.5 %copy.79 = bf16[1,6,8,6,2,32,256]{6,5,4,3,2,1,0:T(8,128)(2,1)} copy(bf16[1,6,8,6,2,32,256]{6,5,4,3,1,2,0:T(8,128)(2,1)} %bitcast.186) | data formatting | bytes 18874368 | tf_op jit(solution)/shard_map/all_to_all | solution.py:78
  388.6 12.0 %fusion.14 = f32[6,2,256,2,256,1]{2,4,5,3,1,0:T(8,128)} fusion(bf16[6,48,2,32,256,1]{4,3,2,1,0,5:T(8,128)(2,1)} %bitcast.188, bf16[1,6,48,2,64,256]{5,4,3,2,1,0:T(8,128)(2,1)} %param.10), kind=kOutput, calls=%fused_computation.32 | convolution fusion | flops 4831838208 | bytes 25165824 | tf_op jit(solution)/shard_map/fijckr,fijeks->fcesir/dot_general | solution.py:79
  420.2 68.0 %all-reduce.2.cloned.1.call-done = bf16[1,2,2,128,128]{4,3,2,1,0:T(8,128)(2,1)} async-done(((bf16[1,2,2,128,128]{4,3,2,1,0:T(8,128)(2,1)}), bf16[1,2,2,128,128]{4,3,2,1,0:T(8,128)(2,1)}) %all-reduce.2.cloned.1.call-update) | async-done | bytes 131088 | tf_op jit(solution)/shard_map/psum | solution.py:132
  (52 shorter events, 37.9 us)
Async XLA Ops:
  49.7 6.6 %copy-start.3 = (s32[1,48,6]{1,0,2:T(1,128)S(1)}, s32[1,48,6]{1,0,2:T(1,128)}, u32[]{:S(2)}) copy-start(s32[1,48,6]{1,0,2:T(1,128)} %param.9) | copy-start | bytes 3460
  52.1 24.3 %all-to-all-start = ((bf16[4,2,2,32,1536]{4,1,3,2,0:T(2,128)(2,1)}), bf16[4,2,2,32,1536]{4,1,3,2,0:T(2,128)(2,1)S(1)}, u32[]{:S(2)}, u32[]{:S(2)}) async-start(bf16[4,2,2,32,1536]{4,1,3,2,0:T(2,128)(2,1)} %copy.70), calls=%async_computation | async-start | bytes 3145728 | tf_op jit(solution)/shard_map/all_to_all | solution.py:65
  137.6 3.6 copy-start
  137.6 6.4 %copy-start.1 = (bf16[1,48,6,1,64,256]{5,4,1,2,3,0:T(8,128)(2,1)}, bf16[1,48,6,1,64,256]{5,4,1,2,3,0:T(8,128)(2,1)S(1)}, u32[]{:S(2)}) copy-start(bf16[1,48,6,1,64,256]{5,4,1,2,3,0:T(8,128)(2,1)S(1)} %get-tuple-element.5) | copy-start | bytes 28311556
  157.0 213.0 %all-to-all-start.1 = ((bf16[1,48,6,2,32,256]{5,4,2,3,0,1:T(8,128)(2,1)}), bf16[1,48,6,2,32,256]{5,4,2,3,0,1:T(8,128)(2,1)}, u32[]{:S(2)}, u32[]{:S(2)}) async-start(bf16[1,48,6,2,32,256]{5,4,2,3,0,1:T(8,128)(2,1)} %copy.77), calls=%async_computation.1 | async-start | bytes 18874368 | tf_op jit(solution)/shard_map/all_to_all | solution.py:78
  163.6 324.5 %all-reduce.2.cloned.1.call-start = ((), (), s32[]{:S(2)}) async-start(), calls=%async_computation.2 | async-start | bytes 262144 | tf_op jit(solution)/shard_map/psum | solution.py:132
  222.5 178.2 %collective-permute-start = (bf16[1,3,1,2,32,256]{5,4,3,2,1,0:T(8,128)(2,1)S(1)}, bf16[1,3,1,2,32,256]{5,4,3,2,1,0:T(8,128)(2,1)S(1)}, u32[]{:S(2)}, u32[]{:S(2)}) collective-permute-start(bf16[1,3,1,2,32,256]{5,4,3,2,1,0:T(8,128)(2,1)S(1)} %get-tuple-element.14), channel_id=1, source_target_pairs={{1,0},{2,1},{3,2},{4,3},{5,4},{6,5},{7,6},{9,8},{10,9},{11,10},{12... | collective-permute-start | bytes 294920 | tf_op jit(solution)/shard_map/ppermute | solution.py:19
  223.8 176.9 %collective-permute-start.1 = (bf16[1,3,1,2,32,256]{5,4,3,2,1,0:T(8,128)(2,1)S(1)}, bf16[1,3,1,2,32,256]{5,4,3,2,1,0:T(8,128)(2,1)S(1)}, u32[]{:S(2)}, u32[]{:S(2)}) collective-permute-start(bf16[1,3,1,2,32,256]{5,4,3,2,1,0:T(8,128)(2,1)S(1)} %get-tuple-element.15), channel_id=1, source_target_pairs={{0,1},{1,2},{2,3},{3,4},{4,5},{5,6},{6,7},{8,9},{9,10},{10,11},{11... | collective-permute-start | bytes 294920 | tf_op jit(solution)/shard_map/ppermute | solution.py:18
  418.7 70.7 %copy-start.2 = (bf16[1,2,128,1536]{3,2,1,0:T(8,128)(2,1)}, bf16[1,2,128,1536]{3,2,1,0:T(8,128)(2,1)S(1)}, u32[]{:S(2)}) copy-start(bf16[1,2,128,1536]{3,2,1,0:T(8,128)(2,1)S(1)} %get-tuple-element.12) | copy-start | bytes 2359300
Sparse Core Ops, SparseCore 0:
  420.3 67.7 all-reduce.1
where the time goes:
time: 498 us; the launch traced here: 496 us
  waiting for transfers between devices  230 us (46%)
  local copies, waits for them, and re-layouts  113 us (23%)
  other arithmetic  67 us (13%)
  matrix products  55.3 us (11%)
  starting transfers between devices  16.7 us (3%)
  between operations  14.3 us (3%)
    all_to_all x1, waiting for transfers between devices, on_device(): lax.all_to_all(lower_part, 'tile', split_axis=1, concat_axis=2, tiled=True)  142 us
    psum x1, waiting for transfers between devices, on_device(): lax.psum(gram_all.astype(jnp.bfloat16), 'tile').astype(jnp.float32)  68 us
    another operation x3, other arithmetic, on_device(): jnp.stack([coeff_real * rank_mask, coeff_imag * rank_mask], 3)  44.6 us
    dot_general x1, matrix products, on_device(): jnp.einsum('fijckr,fdsjr->fijcdks', v_factors, columns, preferred_element...  32.4 us
    gather x3, local copies, waits for them, and re-layouts, on_device(): u_band.append(u_factors[:, row_local, partner][:, :, :, half_depth:])  20.8 us
    gather x3, local copies, waits for them, and re-layouts, on_device(): picked = coeff_all[:, clipped, local_ids][:, :, :, half_depth:]  20.8 us
    all_to_all x1, waiting for transfers between devices, on_device(): lax.all_to_all(local_spec, 'freq', split_axis=0, concat_axis=3, tiled=True)  19.9 us
    broadcast_in_dim x2, local copies, waits for them, and re-layouts, gate_field(): kept = jnp.where(inside, shaped, jnp.zeros((), traces.dtype))  18.7 us
  transfers between devices with their start and end apart: 5, of which 3 were waited for; matrix products, arithmetic and copies ran while one was open for 18% of the time, Pallas kernels for 0%

commit v1 on v0

--- a/solution.py
+++ b/solution.py
@@ -75,7 +75,10 @@
     rank_mask = (rank_ids < tile_ranks[:, :, :, None]).astype(jnp.float32)[..., None]
     coeff_all = jnp.stack([coeff_real * rank_mask, coeff_imag * rank_mask], 3).astype(jnp.bfloat16)
     lower_part = coeff_all[:, :, :, :, :half_depth]
-    lower_rows = lax.all_to_all(lower_part, "tile", split_axis=1, concat_axis=2, tiled=True)
+    peers = lax.axis_size("tile")
+    pieces = jnp.stack(jnp.split(lower_part, peers, axis=1), axis=0)
+    pieces = lax.all_to_all(pieces, "tile", split_axis=0, concat_axis=0)
+    lower_rows = jnp.concatenate(pieces, axis=2)
     products = jnp.einsum(
         "fijckr,fijeks->fcesir",
         u_factors[:, :, :, :, :half_depth],

time: 498 us -> 480 us (0.964)
  local copies, waits for them, and re-layouts: 113 us -> 88.5 us
  other arithmetic: 67 us -> 74.6 us
    all_to_all x2 -> x0, local copies, waits for them, and re-layouts: 18.6 us -> none  [on_device(): lax.all_to_all(lower_part, 'tile', split_axis=1, concat_axis=2, tiled=True)]
    unnamed x0 -> x7, other arithmetic: none -> 10.7 us
    reshape x0 -> x1, local copies, waits for them, and re-layouts: none -> 9.02 us  [on_device(): lower_rows = jnp.concatenate(pieces, axis=2)]
    slice x1 -> x0, local copies, waits for them, and re-layouts: 9 us -> none  [on_device(): lower_part = coeff_all[:, :, :, :, :half_depth]]
    unnamed x10, local copies, waits for them, and re-layouts: 7.14 us -> 0.79 us
    another operation x3 -> x2, other arithmetic: 44.6 us -> 40.5 us  [on_device(): jnp.stack([coeff_real * rank_mask, coeff_imag * rank_mask], 3)]
  transfers between devices with their start and end apart: 5 -> 5, of which waited for: 3 -> 3; matrix products, arithmetic and copies ran while one was open for 18% -> 17% of each run, Pallas kernels for 0% -> 0%
where the time goes in v1:
time: 480 us; the launch traced here: 479 us
  waiting for transfers between devices  229 us (48%)
  local copies, waits for them, and re-layouts  88.5 us (18%)
  other arithmetic  74.6 us (16%)
  matrix products  55.4 us (12%)
  starting transfers between devices  16.9 us (4%)
  between operations  14.3 us (3%)
    all_to_all x1, waiting for transfers between devices, on_device(): pieces = lax.all_to_all(pieces, 'tile', split_axis=0, concat_axis=0)  142 us
    psum x1, waiting for transfers between devices, on_device(): lax.psum(gram_all.astype(jnp.bfloat16), 'tile').astype(jnp.float32)  67.9 us
    another operation x2, other arithmetic, on_device(): jnp.stack([coeff_real * rank_mask, coeff_imag * rank_mask], 3)  40.5 us
    dot_general x1, matrix products, on_device(): jnp.einsum('fijckr,fdsjr->fijcdks', v_factors, columns, preferred_element...  32.4 us
    gather x3, local copies, waits for them, and re-layouts, on_device(): u_band.append(u_factors[:, row_local, partner][:, :, :, half_depth:])  20.8 us
    gather x3, local copies, waits for them, and re-layouts, on_device(): picked = coeff_all[:, clipped, local_ids][:, :, :, half_depth:]  20.8 us
    all_to_all x1, waiting for transfers between devices, on_device(): lax.all_to_all(local_spec, 'freq', split_axis=0, concat_axis=3, tiled=True)  19.9 us
    broadcast_in_dim x2, local copies, waits for them, and re-layouts, gate_field(): kept = jnp.where(inside, shaped, jnp.zeros((), traces.dtype))  18.7 us
  transfers between devices with their start and end apart: 5, of which 3 were waited for; matrix products, arithmetic and copies ran while one was open for 17% of the time, Pallas kernels for 0%

profile of v1, /device:TPU:0, one launch (start us, length us, event | category | flops | bytes accessed | tf_op | source)
XLA Modules:
  0.0 479.1 jit_solution(6255236589496641835)
XLA Ops:
  8.9 4.3 broadcast_in_dim.81
  13.2 14.4 %copy.46 = pred[32,128,1536]{2,1,0:T(8,128)(4,1)} copy(pred[32,128,1536]{1,2,0:T(8,128)(4,1)} %bitcast.200) | data formatting | bytes 12582912 | tf_op jit(solution)/shard_map/jit(_where)/broadcast_in_dim | solution.py:47
  27.6 15.3 %select_bitcast_fusion.1 = (bf16[1,32,128,1536]{3,2,1,0:T(8,128)(2,1)S(1)}, bf16[1,32,128,1536]{3,2,1,0:T(8,128)(2,1)}) fusion(pred[32,128,1536]{2,1,0:T(8,128)(4,1)} %copy.46, bf16[32,128,1536]{2,1,0:T(8,128)(2,1)} %param.6, bf16[32,128,1536]{2,1,0:T(8,128)(2,1)} %param.7), kind=kLoop, calls=%fused_computation.41 | loop fusion | flops 12582912 | bytes 56623104 | tf_op jit(solution)/shard_map/jit(_where)/select_n | solution.py:47
  42.9 6.8 %fusion.17 = bf16[4,2,2,32,1536]{4,0,1,3,2:T(4,128)(2,1)S(1)} fusion(bf16[1,32,128,1536]{3,2,1,0:T(8,128)(2,1)} %get-tuple-element.11, bf16[1,32,128,1536]{3,2,1,0:T(8,128)(2,1)S(1)} %get-tuple-element.10, bf16[1,4,128]{2,1,0:T(4,128)(2,1)S(1)} %get-tuple-element.24, bf16[1,4,128]{2,1,0:T(4,128)(2,1)S(1)} %get-tuple-element.25), kind=kOutput, calls=%fused_computation.50 | convolution fusion | flops 252448768 | bytes 26740736 | tf_op jit(solution)/shard_map/cft,qstr->fcqsr/dot_general | solution.py:62
  52.1 4.2 all-to-all-start
  56.5 19.9 %all-to-all-done = bf16[4,2,2,32,1536]{4,1,3,2,0:T(2,128)(2,1)S(1)} async-done(((bf16[4,2,2,32,1536]{4,1,3,2,0:T(2,128)(2,1)}), bf16[4,2,2,32,1536]{4,1,3,2,0:T(2,128)(2,1)S(1)}, u32[]{:S(2)}, u32[]{:S(2)}) %all-to-all-start) | async-done | bytes 1572896 | tf_op jit(solution)/shard_map/all_to_all | solution.py:65
  77.8 3.3 reshape.602
  81.1 32.4 %convolution_bitcast_fusion = f32[1,48,6,2,2,64,256]{6,5,3,1,4,2,0:T(8,128)} fusion(bf16[2,256,6,256,1,1]{3,2,1,0,5,4:T(8,128)(2,1)S(1)} %bitcast.202, bf16[1,48,6,2,64,256]{5,4,3,2,1,0:T(8,128)(2,1)} %param.11), kind=kOutput, calls=%fused_computation.23 | convolution fusion | flops 9663676416 | bytes 95944704 | tf_op jit(solution)/shard_map/fijckr,fdsjr->fijcdks/dot_general | solution.py:69
  113.5 24.0 %fusion.11 = (bf16[1,48,6,1,64,256]{5,4,1,2,3,0:T(8,128)(2,1)S(1)}, bf16[1,48,6,1,64,256]{5,4,1,2,3,0:T(8,128)(2,1)S(1)}) fusion(f32[1,48,6,2,2,64,256]{6,5,3,1,4,2,0:T(8,128)} %convolution_bitcast_fusion, f32[48,6,64]{2,0,1:T(8,128)S(1)} %fusion.56, f32[256]{0:T(256)S(1)} %compare_select_fusion.4), kind=kLoop, calls=%fused_computation.42 | loop fusion | flops 37748736 | bytes 94446592 | tf_op jit(solution)/shard_map/stack | solution.py:76
  149.3 6.6 %all-to-all-start.1 = ((bf16[8,1,6,6,2,32,256]{6,5,2,3,4,1,0:T(8,128)(2,1)}), bf16[8,1,6,6,2,32,256]{6,5,2,3,4,1,0:T(8,128)(2,1)}, u32[]{:S(2)}, u32[]{:S(2)}) async-start(bf16[8,1,6,6,2,32,256]{6,5,2,3,4,1,0:T(8,128)(2,1)} %bitcast_dynamic-update-slice_fusion), calls=%async_computation.1 | async-start | bytes 18874368 | tf_op jit(solution)/shard_map/all_to_all | solution.py:80
  156.2 6.9 %gather_fusion.5 = bf16[6,2,64,256]{3,2,1,0:T(8,128)(2,1)S(1)} fusion(bf16[6,48,2,64,256]{4,3,2,1,0:T(8,128)(2,1)} %bitcast.218, s32[6]{0:T(128)S(1)} %get-tuple-element.28), kind=kCustom, calls=%fused_computation.5 | custom fusion | bytes 786480 | tf_op jit(solution)/shard_map/gather | solution.py:111
  163.2 6.9 %gather_fusion.4 = bf16[6,2,64,256]{3,2,1,0:T(8,128)(2,1)S(1)} fusion(bf16[6,48,2,64,256]{4,3,2,1,0:T(8,128)(2,1)} %bitcast.219, s32[6]{0:T(128)S(1)} %get-tuple-element.29), kind=kCustom, calls=%fused_computation.4 | custom fusion | bytes 786480 | tf_op jit(solution)/shard_map/gather | solution.py:111
  170.1 6.9 %gather_fusion.3 = bf16[6,2,64,256]{3,2,1,0:T(8,128)(2,1)S(1)} fusion(bf16[6,48,2,64,256]{4,3,2,1,0:T(8,128)(2,1)} %bitcast.220, s32[6]{0:T(128)S(1)} %get-tuple-element.30), kind=kCustom, calls=%fused_computation.3 | custom fusion | bytes 786480 | tf_op jit(solution)/shard_map/gather | solution.py:111
  177.2 16.5 %fusion.1 = bf16[48,6,2,64,256]{4,3,0,1,2:T(8,128)(2,1)} fusion(bf16[1,48,6,1,64,256]{5,4,1,2,3,0:T(8,128)(2,1)} %copy-done.1, bf16[1,48,6,1,64,256]{5,4,1,2,3,0:T(8,128)(2,1)} %copy-done), kind=kLoop, calls=%fused_computation.26 | loop fusion | flops 9437184 | bytes 37748736 | tf_op jit(solution)/shard_map/stack | solution.py:76
  193.7 6.9 %gather_fusion.2 = bf16[6,2,64,256]{3,2,1,0:T(8,128)(2,1)S(1)} fusion(bf16[48,6,2,64,256]{4,3,0,1,2:T(8,128)(2,1)} %fusion.1, s32[6]{0:T(128)S(1)} %get-tuple-element.31), kind=kCustom, calls=%fused_computation.2 | custom fusion | bytes 786480 | tf_op jit(solution)/shard_map/gather | solution.py:96
  200.7 6.9 %gather_fusion.1 = bf16[6,2,64,256]{3,2,1,0:T(8,128)(2,1)S(1)} fusion(bf16[48,6,2,64,256]{4,3,0,1,2:T(8,128)(2,1)} %fusion.1, s32[6]{0:T(128)S(1)} %get-tuple-element.32), kind=kCustom, calls=%fused_computation.1 | custom fusion | bytes 786480 | tf_op jit(solution)/shard_map/gather | solution.py:96
  207.6 6.9 %gather_fusion = bf16[6,2,64,256]{3,2,1,0:T(8,128)(2,1)S(1)} fusion(bf16[48,6,2,64,256]{4,3,0,1,2:T(8,128)(2,1)} %fusion.1, s32[6]{0:T(128)S(1)} %get-tuple-element.33), kind=kCustom, calls=%fused_computation | custom fusion | bytes 786480 | tf_op jit(solution)/shard_map/gather | solution.py:96
  216.3 4.6 collective-permute-start.1
  220.8 141.5 %all-to-all-done.1 = bf16[8,1,6,6,2,32,256]{6,5,2,3,4,1,0:T(8,128)(2,1)} async-done(((bf16[8,1,6,6,2,32,256]{6,5,2,3,4,1,0:T(8,128)(2,1)}), bf16[8,1,6,6,2,32,256]{6,5,2,3,4,1,0:T(8,128)(2,1)}, u32[]{:S(2)}, u32[]{:S(2)}) %all-to-all-start.1) | async-done | bytes 9437216 | tf_op jit(solution)/shard_map/all_to_all | solution.py:80
  362.3 9.0 %copy.55 = bf16[1,6,8,6,2,32,256]{6,5,4,3,2,1,0:T(8,128)(2,1)} copy(bf16[1,6,8,6,2,32,256]{6,5,1,3,4,0,2:T(8,128)(2,1)} %bitcast.30) | data formatting | bytes 18874368 | tf_op jit(solution)/shard_map/reshape | solution.py:81
  371.4 12.0 %fusion.13 = f32[6,2,256,2,256,1]{2,4,5,3,1,0:T(8,128)} fusion(bf16[6,48,2,32,256,1]{4,3,2,1,0,5:T(8,128)(2,1)} %bitcast.201, bf16[1,6,48,2,64,256]{5,4,3,2,1,0:T(8,128)(2,1)} %param.10), kind=kOutput, calls=%fused_computation.45 | convolution fusion | flops 4831838208 | bytes 25165824 | tf_op jit(solution)/shard_map/fijckr,fijeks->fcesir/dot_general | solution.py:82
  383.4 3.5 fusion.15
  397.3 3.1 add_convert_fusion
  403.0 67.9 %all-reduce.2.cloned.1.call-done = bf16[1,2,2,128,128]{4,3,2,1,0:T(8,128)(2,1)} async-done(((bf16[1,2,2,128,128]{4,3,2,1,0:T(8,128)(2,1)}), bf16[1,2,2,128,128]{4,3,2,1,0:T(8,128)(2,1)}) %all-reduce.2.cloned.1.call-update) | async-done | bytes 131088 | tf_op jit(solution)/shard_map/psum | solution.py:135
  (57 shorter events, 33.5 us)
Async XLA Ops:
  49.7 6.6 %copy-start.3 = (s32[1,48,6]{1,0,2:T(1,128)S(1)}, s32[1,48,6]{1,0,2:T(1,128)}, u32[]{:S(2)}) copy-start(s32[1,48,6]{1,0,2:T(1,128)} %param.9) | copy-start | bytes 3460
  52.1 24.3 %all-to-all-start = ((bf16[4,2,2,32,1536]{4,1,3,2,0:T(2,128)(2,1)}), bf16[4,2,2,32,1536]{4,1,3,2,0:T(2,128)(2,1)S(1)}, u32[]{:S(2)}, u32[]{:S(2)}) async-start(bf16[4,2,2,32,1536]{4,1,3,2,0:T(2,128)(2,1)} %copy.48), calls=%async_computation | async-start | bytes 3145728 | tf_op jit(solution)/shard_map/all_to_all | solution.py:65
  137.6 10.7 %copy-start = (bf16[1,48,6,1,64,256]{5,4,1,2,3,0:T(8,128)(2,1)}, bf16[1,48,6,1,64,256]{5,4,1,2,3,0:T(8,128)(2,1)S(1)}, u32[]{:S(2)}) copy-start(bf16[1,48,6,1,64,256]{5,4,1,2,3,0:T(8,128)(2,1)S(1)} %get-tuple-element.4) | copy-start | bytes 28311556
  137.6 10.7 %copy-start.1 = (bf16[1,48,6,1,64,256]{5,4,1,2,3,0:T(8,128)(2,1)}, bf16[1,48,6,1,64,256]{5,4,1,2,3,0:T(8,128)(2,1)S(1)}, u32[]{:S(2)}) copy-start(bf16[1,48,6,1,64,256]{5,4,1,2,3,0:T(8,128)(2,1)S(1)} %get-tuple-element.5) | copy-start | bytes 28311556
  149.3 213.0 %all-to-all-start.1 = ((bf16[8,1,6,6,2,32,256]{6,5,2,3,4,1,0:T(8,128)(2,1)}), bf16[8,1,6,6,2,32,256]{6,5,2,3,4,1,0:T(8,128)(2,1)}, u32[]{:S(2)}, u32[]{:S(2)}) async-start(bf16[8,1,6,6,2,32,256]{6,5,2,3,4,1,0:T(8,128)(2,1)} %bitcast_dynamic-update-slice_fusion), calls=%async_computation.1 | async-start | bytes 18874368 | tf_op jit(solution)/shard_map/all_to_all | solution.py:80
  156.0 315.0 %all-reduce.2.cloned.1.call-start = ((), (), s32[]{:S(2)}) async-start(), calls=%async_computation.2 | async-start | bytes 262144 | tf_op jit(solution)/shard_map/psum | solution.py:135
  215.0 168.4 %collective-permute-start = (bf16[1,3,1,2,32,256]{5,4,3,2,1,0:T(8,128)(2,1)S(1)}, bf16[1,3,1,2,32,256]{5,4,3,2,1,0:T(8,128)(2,1)S(1)}, u32[]{:S(2)}, u32[]{:S(2)}) collective-permute-start(bf16[1,3,1,2,32,256]{5,4,3,2,1,0:T(8,128)(2,1)S(1)} %get-tuple-element.14), channel_id=1, source_target_pairs={{1,0},{2,1},{3,2},{4,3},{5,4},{6,5},{7,6},{9,8},{10,9},{11,10},{12... | collective-permute-start | bytes 294920 | tf_op jit(solution)/shard_map/ppermute | solution.py:19
  216.3 167.1 %collective-permute-start.1 = (bf16[1,3,1,2,32,256]{5,4,3,2,1,0:T(8,128)(2,1)S(1)}, bf16[1,3,1,2,32,256]{5,4,3,2,1,0:T(8,128)(2,1)S(1)}, u32[]{:S(2)}, u32[]{:S(2)}) collective-permute-start(bf16[1,3,1,2,32,256]{5,4,3,2,1,0:T(8,128)(2,1)S(1)} %get-tuple-element.15), channel_id=1, source_target_pairs={{0,1},{1,2},{2,3},{3,4},{4,5},{5,6},{6,7},{8,9},{9,10},{10,11},{11... | collective-permute-start | bytes 294920 | tf_op jit(solution)/shard_map/ppermute | solution.py:18
  401.5 70.7 %copy-start.2 = (bf16[1,2,128,1536]{3,2,1,0:T(8,128)(2,1)}, bf16[1,2,128,1536]{3,2,1,0:T(8,128)(2,1)S(1)}, u32[]{:S(2)}) copy-start(bf16[1,2,128,1536]{3,2,1,0:T(8,128)(2,1)S(1)} %get-tuple-element.12) | copy-start | bytes 2359300
Sparse Core Ops, SparseCore 0:
  403.1 67.7 all-reduce.1
